TPU v7x, 256 devices: a whole 4x4x8 slice. The times are simulated.
256 devices in a mesh: item: 32 (over x, z), day: 8 (over y, core).
Axes of the slice: x: 4, y: 4, z: 8, core: 2. Of those that a mesh axis runs over, the one named last changes fastest.
Arguments:
- user_factors: float32 [2048, 512], P(('item', 'day')), may hold values from 0.005 to 0.012
- item_factors: bfloat16 [16384, 512], P('item'), may hold values from 0 to 1
- day_factors: bfloat16 [368, 512], P('day'), may hold values from 0.099609375 to 1
- tile_counts: bfloat16 [32768, 128, 128], P(('item', 'day')), may hold values from 0 to 23
- tile_index: int32 [3, 32768], P(None, ('item', 'day')), may hold values from 0 to 45, as said below
- tile_live: int32 [256], P(('item', 'day')), may hold values from 32 to 128, as said below
Outputs:
- updated_users: float32 [2048, 512], P(('item', 'day'))
Inputs may be any that keep to these rules, and one draw needn't show every extreme that they name: `tile_index`: row 0 names a user block below 16, row 1 an item block below 4 and row 2 a day below 46, local to the device that holds the slot. Only the first tile_live[d] slots of list d are live; some list has all 128 live.
All inputs are finite; a program needn't handle non-finite values.
Results may differ from a plain program's by a relative error of at most 0.003.
Values may be sent and summed in bfloat16 or wider, within the bound.
A program may use at most 64 MiB of HBM per device.

v0:
```python
import jax
import jax.numpy as jnp
from jax import lax
from jax.sharding import PartitionSpec as P

TILE = 128
GROUP = 8


def group_turns(phi, user_blocks, item_blocks, day_rows, counts, index, low, high):

    def turn(step, phi):
        start = step * GROUP
        tile_vals = lax.dynamic_slice_in_dim(counts, start, GROUP, 0)
        picks = lax.dynamic_slice_in_dim(index, start, GROUP, 1)
        places = start + jnp.arange(GROUP, dtype=jnp.int32)
        active = (places >= low) & (places < high)
        users = user_blocks[picks[0]]
        items = item_blocks[picks[1]]
        scales = day_rows[picks[2]].astype(jnp.float32)[:, None, :]
        scaled = (users.astype(jnp.float32) * scales).astype(jnp.bfloat16)
        model = jnp.einsum("gur,gir->gui", scaled, items, preferred_element_type=jnp.float32)
        ratio = jnp.where(active[:, None, None], tile_vals.astype(jnp.float32) / model, 0.0).astype(
            jnp.bfloat16
        )
        weighted = (items.astype(jnp.float32) * scales).astype(jnp.bfloat16)
        terms = jnp.einsum("gui,gir->gur", ratio, weighted, preferred_element_type=jnp.float32)
        return phi.at[picks[0]].add(terms)

    first = jnp.maximum(low, 0) // GROUP
    last = jnp.maximum((high + GROUP - 1) // GROUP, first)
    return lax.fori_loop(first, last, turn, phi)


def per_device(user_factors, item_factors, day_factors, tile_counts, tile_index, tile_live):
    rank = user_factors.shape[1]
    gathered = lax.all_gather(
        user_factors.astype(jnp.bfloat16), ("item", "day"), axis=0, tiled=True
    )
    user_blocks = gathered.reshape(-1, TILE, rank)
    item_blocks = item_factors.reshape(-1, TILE, rank)
    phi = jnp.zeros(user_blocks.shape, jnp.float32)
    own_count = tile_live[0]
    phi = group_turns(
        phi, user_blocks, item_blocks, day_factors, tile_counts, tile_index, 0, own_count
    )
    owned = lax.psum_scatter(
        phi.reshape(-1, rank), ("item", "day"), scatter_dimension=0, tiled=True
    )
    item_total = lax.psum(jnp.sum(item_factors.astype(jnp.float32), axis=0), "item")
    day_total = lax.psum(jnp.sum(day_factors.astype(jnp.float32), axis=0), "day")
    return user_factors * owned / (item_total * day_total)


def solution(mesh):
    in_specs = (
        P(("item", "day"), None),
        P("item", None),
        P("day", None),
        P(("item", "day"), None, None),
        P(None, ("item", "day")),
        P(("item", "day")),
    )
    out_specs = P(("item", "day"), None)
    return jax.shard_map(
        per_device, mesh=mesh, in_specs=in_specs, out_specs=out_specs, check_vma=False
    )
```

profile of v0, /device:TPU:0, one launch (start us, length us, event | category | flops | bytes accessed | tf_op | source)
XLA Modules:
  0.0 1605.5 jit_solution(8117053464810953249)
XLA Ops:
  8.6 107.7 %all-gather.2.cloned.1.call-done = bf16[2048,512]{1,0:T(8,128)(2,1)} async-done(((bf16[8,512]{1,0:T(8,128)(2,1)}), bf16[2048,512]{1,0:T(8,128)(2,1)}) %all-gather.2.cloned.1.call-update) | async-done | bytes 2097168 | tf_op jit(solution)/shard_map/all_gather | solution.py:37
  118.7 104.4 %while.10 = (s32[]{:T(128)}, f32[16,128,512]{2,1,0:T(8,128)}, s32[]{:T(128)}, s32[3,128]{1,0:T(4,128)S(1)}, s32[]{:T(128)}, /*index=5*/bf16[128,128,128]{2,1,0:T...) while((s32[]{:T(128)}, f32[16,128,512]{2,1,0:T(8,128)}, ...), condition=%wide.region_2.3_spmd, body=%wide.region_0.2_spmd.sunk | while | flops 272637024 | bytes 16078115 | solution.py:32
  121.1 3.2 gather_fusion.1
  127.6 4.1 scatter_fusion
  134.0 3.2 gather_fusion.1
  140.6 4.3 scatter_fusion
  147.1 3.2 gather_fusion.1
  153.7 4.2 scatter_fusion
  160.2 3.2 gather_fusion.1
  166.7 4.2 scatter_fusion
  173.2 3.2 gather_fusion.1
  177.0 2.7 fusion.20
  179.7 4.3 scatter_fusion
  186.3 3.2 gather_fusion.1
  192.8 4.2 scatter_fusion
  199.3 3.2 gather_fusion.1
  203.1 2.7 fusion.20
  205.8 4.2 scatter_fusion
  212.3 3.2 gather_fusion.1
  216.2 2.7 fusion.20
  218.9 4.2 scatter_fusion
  223.2 74.5 %psum.14 = f32[512]{0:T(512)S(1)} all-reduce(f32[512]{0:T(512)S(1)} %convert_reduce_fusion), channel_id=1, replica_groups=mesh['item'=32,'day'=8] {'item'}, use_global_device_ids=true, to_apply=%region_5.6 | all-reduce | flops 512 | bytes 4096 | tf_op jit(solution)/shard_map/psum | solution.py:50
  297.8 95.0 %psum.15 = f32[512]{0:T(512)S(1)} all-reduce(f32[512]{0:T(512)S(1)} %convert_reduce_fusion.1), channel_id=1, replica_groups=mesh['item'=32,'day'=8] {'day'}, use_global_device_ids=true, to_apply=%region_7.8 | all-reduce | flops 512 | bytes 4096 | tf_op jit(solution)/shard_map/psum | solution.py:51
  392.8 1204.5 %reduce-scatter.2.cloned.1.call-done = f32[8,512]{1,0:T(8,128)} async-done(((f32[2048,512]{1,0:T(8,128)}), f32[8,512]{1,0:T(8,128)}) %reduce-scatter.2.cloned.1.call-update) | async-done | bytes 16400 | tf_op jit(solution)/shard_map/reduce_scatter | solution.py:47
  (87 shorter events, 42.3 us)
Async XLA Ops:
  6.5 109.7 %all-gather.2.cloned.1.call-start = ((), (), s32[]{:S(2)}) async-start(), calls=%async_computation.1 | async-start | bytes 2105344 | tf_op jit(solution)/shard_map/all_gather | solution.py:37
  7.9 1589.4 %reduce-scatter.2.cloned.1.call-start = ((), (), s32[]{:S(2)}) async-start(), calls=%async_computation.2 | async-start | bytes 4210688 | tf_op jit(solution)/shard_map/reduce_scatter | solution.py:47
  116.3 2.5 copy-start
  116.3 2.5 copy-start.1
  116.3 2.5 copy-start.3
  223.1 1374.2 %copy-start.2 = (f32[8,512]{1,0:T(8,128)S(1)}, f32[8,512]{1,0:T(8,128)}, u32[]{:S(2)}) copy-start(f32[8,512]{1,0:T(8,128)} %param.8) | copy-start | bytes 49156
Sparse Core Ops, SparseCore 0:
  11.1 105.1 all-gather.1
  223.2 1374.0 reduce-scatter.1
where the time goes:
time: 1610 us
  waiting for transfers between devices  1310 us (81%)
  blocking collectives  170 us (11%)
  local copies, waits for them, and re-layouts  46 us (3%)
  other arithmetic  41.9 us (3%)
  matrix products  21.5 us (1%)
    reduce_scatter x1, waiting for transfers between devices, per_device(): lax.psum_scatter(phi.reshape(-1, rank), ('item', 'day'), scatter_dimensio...  1200 us
    all_gather x1, waiting for transfers between devices, per_device(): lax.all_gather(user_factors.astype(jnp.bfloat16), ('item', 'day'), axis=0...  108 us
    psum x1, blocking collectives, per_device(): lax.psum(jnp.sum(day_factors.astype(jnp.float32), axis=0), 'day')  95 us
    psum x1, blocking collectives, per_device(): lax.psum(jnp.sum(item_factors.astype(jnp.float32), axis=0), 'item')  74.5 us
    scatter-add x8, other arithmetic, turn(): return phi.at[picks[0]].add(terms)  33.7 us
  transfers between devices with their start and end apart: 2, of which 2 were waited for; matrix products, arithmetic and copies ran while one was open for 0% of the time, Pallas kernels for 0%

commit v1 on v0

--- a/solution.py
+++ b/solution.py
@@ -34,8 +34,14 @@
 
 def per_device(user_factors, item_factors, day_factors, tile_counts, tile_index, tile_live):
     rank = user_factors.shape[1]
-    gathered = lax.all_gather(
-        user_factors.astype(jnp.bfloat16), ("item", "day"), axis=0, tiled=True
+    gathered = jnp.concatenate(
+        lax.all_to_all(
+            jnp.stack([user_factors.astype(jnp.bfloat16)] * lax.axis_size(("item", "day"))),
+            ("item", "day"),
+            0,
+            0,
+        ),
+        axis=0,
     )
     user_blocks = gathered.reshape(-1, TILE, rank)
     item_blocks = item_factors.reshape(-1, TILE, rank)

time: 1610 us -> 1560 us (0.969)
  waiting for transfers between devices: 1310 us -> 1260 us
    all_gather x1 -> x0, waiting for transfers between devices: 108 us -> none  [per_device(): lax.all_gather(user_factors.astype(jnp.bfloat16), ('item', 'day'), axis=0...]
    all_to_all x0 -> x1, waiting for transfers between devices: none -> 50.3 us  [per_device(): lax.all_to_all(jnp.stack([user_factors.astype(jnp.bfloat16)] * lax.axis_s...]
where the time goes in v1:
time: 1560 us
  waiting for transfers between devices  1260 us (81%)
  blocking collectives  167 us (11%)
  local copies, waits for them, and re-layouts  47.5 us (3%)
  other arithmetic  41.3 us (3%)
  matrix products  21.5 us (1%)
  starting transfers between devices  15.7 us (1%)
    reduce_scatter x1, waiting for transfers between devices, per_device(): lax.psum_scatter(phi.reshape(-1, rank), ('item', 'day'), scatter_dimensio...  1200 us
    psum x1, blocking collectives, per_device(): lax.psum(jnp.sum(day_factors.astype(jnp.float32), axis=0), 'day')  96.5 us
    psum x1, blocking collectives, per_device(): lax.psum(jnp.sum(item_factors.astype(jnp.float32), axis=0), 'item')  70.2 us
    all_to_all x1, waiting for transfers between devices, per_device(): lax.all_to_all(jnp.stack([user_factors.astype(jnp.bfloat16)] * lax.axis_s...  50.3 us
    scatter-add x8, other arithmetic, turn(): return phi.at[picks[0]].add(terms)  33.7 us
  transfers between devices with their start and end apart: 2, of which 2 were waited for; matrix products, arithmetic and copies ran while one was open for 0% of the time, Pallas kernels for 0%

profile of v1, /device:TPU:0, one launch (start us, length us, event | category | flops | bytes accessed | tf_op | source)
XLA Modules:
  0.0 1562.2 jit_solution(9244035109112738977)
XLA Ops:
  8.7 15.6 %all-to-all-start = ((bf16[256,8,512]{2,1,0:T(8,128)(2,1)}), bf16[256,8,512]{2,1,0:T(8,128)(2,1)}, u32[]{:S(2)}, u32[]{:S(2)}) async-start(bf16[256,8,512]{2,1,0:T(8,128)(2,1)} %stack.2), calls=%async_computation | async-start | bytes 4194304 | tf_op jit(solution)/shard_map/all_to_all | solution.py:38
  25.1 50.3 %all-to-all-done = bf16[256,8,512]{2,1,0:T(8,128)(2,1)} async-done(((bf16[256,8,512]{2,1,0:T(8,128)(2,1)}), bf16[256,8,512]{2,1,0:T(8,128)(2,1)}, u32[]{:S(2)}, u32[]{:S(2)}) %all-to-all-start) | async-done | bytes 2097184 | tf_op jit(solution)/shard_map/all_to_all | solution.py:38
  77.9 104.4 %while.10 = (s32[]{:T(128)}, f32[16,128,512]{2,1,0:T(8,128)}, s32[]{:T(128)}, s32[3,128]{1,0:T(4,128)S(1)}, s32[]{:T(128)}, /*index=5*/bf16[128,128,128]{2,1,0:T...) while((s32[]{:T(128)}, f32[16,128,512]{2,1,0:T(8,128)}, ...), condition=%wide.region_2.3_spmd, body=%wide.region_0.2_spmd.sunk | while | flops 272637024 | bytes 16078115 | solution.py:32
  80.2 3.2 gather_fusion.1
  86.8 4.1 scatter_fusion
  93.2 3.2 gather_fusion.1
  99.7 4.3 scatter_fusion
  106.3 3.2 gather_fusion.1
  112.8 4.2 scatter_fusion
  119.4 3.2 gather_fusion.1
  123.2 2.7 fusion.20
  125.9 4.2 scatter_fusion
  132.4 3.2 gather_fusion.1
  136.2 2.7 fusion.20
  138.9 4.3 scatter_fusion
  145.5 3.2 gather_fusion.1
  152.0 4.2 scatter_fusion
  158.5 3.2 gather_fusion.1
  165.0 4.2 scatter_fusion
  171.5 3.2 gather_fusion.1
  178.1 4.2 scatter_fusion
  182.4 70.2 %psum.14 = f32[512]{0:T(512)S(1)} all-reduce(f32[512]{0:T(512)S(1)} %convert_reduce_fusion), channel_id=1, replica_groups=mesh['item'=32,'day'=8] {'item'}, use_global_device_ids=true, to_apply=%region_5.6 | all-reduce | flops 512 | bytes 4096 | tf_op jit(solution)/shard_map/psum | solution.py:56
  252.7 96.5 %psum.15 = f32[512]{0:T(512)S(1)} all-reduce(f32[512]{0:T(512)S(1)} %convert_reduce_fusion.1), channel_id=1, replica_groups=mesh['item'=32,'day'=8] {'day'}, use_global_device_ids=true, to_apply=%region_7.8 | all-reduce | flops 512 | bytes 4096 | tf_op jit(solution)/shard_map/psum | solution.py:57
  349.2 1204.8 %reduce-scatter.2.cloned.1.call-done = f32[8,512]{1,0:T(8,128)} async-done(((f32[2048,512]{1,0:T(8,128)}), f32[8,512]{1,0:T(8,128)}) %reduce-scatter.2.cloned.1.call-update) | async-done | bytes 16400 | tf_op jit(solution)/shard_map/reduce_scatter | solution.py:53
  (87 shorter events, 45.8 us)
Async XLA Ops:
  8.7 66.7 %all-to-all-start = ((bf16[256,8,512]{2,1,0:T(8,128)(2,1)}), bf16[256,8,512]{2,1,0:T(8,128)(2,1)}, u32[]{:S(2)}, u32[]{:S(2)}) async-start(bf16[256,8,512]{2,1,0:T(8,128)(2,1)} %stack.2), calls=%async_computation | async-start | bytes 4194304 | tf_op jit(solution)/shard_map/all_to_all | solution.py:38
  24.4 1529.7 %reduce-scatter.2.cloned.1.call-start = ((), (), s32[]{:S(2)}) async-start(), calls=%async_computation.2 | async-start | bytes 4210688 | tf_op jit(solution)/shard_map/reduce_scatter | solution.py:53
  75.4 2.5 copy-start
  75.4 2.5 copy-start.1
  75.4 2.5 copy-start.3
  182.3 1371.8 %copy-start.2 = (f32[8,512]{1,0:T(8,128)S(1)}, f32[8,512]{1,0:T(8,128)}, u32[]{:S(2)}) copy-start(f32[8,512]{1,0:T(8,128)} %param.8) | copy-start | bytes 49156
Sparse Core Ops, SparseCore 0:
  182.4 1371.5 reduce-scatter.1
